TPU v7x, 256 devices: a whole 4x4x8 slice. The times are simulated.
256 devices in a mesh: ctx: 32 (over y_hi, z, core), exp: 8 (over x, y_lo).
Axes of the slice: x: 4, y: 4 (y_hi: 2, y_lo: 2; y = y_hi * 2 + y_lo), z: 8, core: 2. Of those that a mesh axis runs over, the one named last changes fastest.
Arguments:
- queries: bfloat16 [4096, 6144], P('ctx', 'exp'), may hold values from -12 to 12
- keys_values: bfloat16 [4096, 8, 256], P('ctx', 'exp'), may hold values from -12 to 12
- doc_ids: int32 [4096], P('ctx'), may hold values from 0 to 7, never falling along the last dimension, each value on 1 to 3072 neighbouring positions
- gate_up: bfloat16 [8, 1280, 16384], P('exp', None, 'ctx'), may hold values from -6 to 6
- down_weight: bfloat16 [8, 16384, 6144], P('exp', 'ctx'), may hold values from -0.046875 to 0.046875
- routes: int32 [4096, 2], P(('ctx', 'exp')), may hold values from 0 to 7, all different within a row; in each aligned block of 16 rows (0 to 15, 16 to 31, ...) at most 5 rows name the same one
- route_weights: float32 [4096, 2], P(('ctx', 'exp')), may hold values from 0.1 to 1
Outputs:
- context: bfloat16 [4096, 6144], P('ctx', 'exp')
- moe_out: bfloat16 [4096, 6144], P(('ctx', 'exp'))
Inputs may be any that keep to these rules, and one draw needn't show every extreme that they name: doc_ids never falls along the sequence; each document has 1 to 3072 tokens and one has exactly 3072. `routes`: the 2 experts of a token differ; among the 16 tokens of one device (aligned blocks) no expert is named more than 5 times, a bound that some block reaches.
All inputs are finite; a program needn't handle non-finite values.
Results may differ from a plain program's by a relative error of at most 0.025.
Values may be sent and summed in bfloat16 or wider, within the bound.
No kernel may reach another device: no remote copies, remote signals or barrier semaphores. Data moves between devices by JAX's collectives and lax.ppermute only.
A program may use at most 128 MiB of HBM per device.

v0:
```python
import math
import jax
import jax.numpy as jnp
from jax import lax
from jax.sharding import PartitionSpec as P


def shards(queries, keys_values, doc_ids, gate_up, down_weight, routes, route_weights):
    tok_rows = queries.shape[0]
    local_heads = keys_values.shape[1]
    head_size = keys_values.shape[2] // 2
    groups = queries.shape[1] // (local_heads * head_size)
    query_grid = queries.reshape(tok_rows, local_heads, groups, head_size)
    first_pos = lax.axis_index("ctx") * tok_rows
    query_pos = first_pos + jnp.arange(tok_rows, dtype=jnp.int32)
    scale = 1.0 / math.sqrt(head_size)
    doc_wire = doc_ids.astype(jnp.bfloat16)
    kv_piece = lax.all_gather(keys_values, "ctx", axis=0, tiled=True)
    doc_piece = lax.all_gather(doc_wire, "ctx", axis=0, tiled=True)
    count = kv_piece.shape[0]
    key_pos = jnp.arange(count, dtype=jnp.int32)
    scores = (
        jnp.einsum(
            "qhgd,khd->hgqk",
            query_grid,
            kv_piece[:, :, :head_size],
            preferred_element_type=jnp.float32,
        )
        * scale
    )
    allowed = (doc_ids[:, None] == doc_piece.astype(jnp.int32)[None, :]) & (
        key_pos[None, :] <= query_pos[:, None]
    )
    scores = jnp.where(allowed, scores, jnp.float32(-1e30))
    run_max = jnp.full((local_heads, groups, tok_rows), -1e30, jnp.float32)
    new_max = jnp.maximum(run_max, jnp.max(scores, axis=-1))
    weights = jnp.where(allowed, jnp.exp(scores - new_max[..., None]), jnp.float32(0.0))
    new_total = jnp.sum(weights, axis=-1)
    update = jnp.einsum(
        "hgqk,khd->qhgd",
        weights.astype(jnp.bfloat16),
        kv_piece[:, :, head_size:],
        preferred_element_type=jnp.float32,
    )
    context = (
        (update / jnp.transpose(new_total, (2, 0, 1))[..., None])
        .reshape(tok_rows, -1)
        .astype(jnp.bfloat16)
    )
    residual = lax.all_to_all(context, "exp", split_axis=0, concat_axis=1, tiled=True)
    acts = gate_up[0]
    weight = down_weight[0]
    slot_total = acts.shape[0]
    ctx_count = lax.axis_size("ctx")
    exp_count = lax.axis_size("exp")
    capacity = slot_total // (ctx_count * exp_count)
    width = weight.shape[1]
    mine = lax.psum_scatter(
        jnp.dot(acts, weight, preferred_element_type=jnp.float32).astype(jnp.bfloat16),
        "ctx",
        scatter_dimension=0,
        tiled=True,
    ).astype(jnp.float32)
    mine = mine.astype(jnp.bfloat16).reshape(exp_count, capacity, width)
    home_rows = lax.all_to_all(mine, "exp", split_axis=0, concat_axis=0, tiled=True)
    expert_count = home_rows.shape[0]
    flat_routes = routes.reshape(-1)
    onehot = (flat_routes[:, None] == jnp.arange(expert_count, dtype=jnp.int32)[None, :]).astype(
        jnp.int32
    )
    earlier = jnp.cumsum(onehot, axis=0) - onehot
    slot_index = jnp.sum(earlier * onehot, axis=1)
    row_index = flat_routes * capacity + slot_index
    picked = home_rows.reshape(expert_count * capacity, width)[row_index]
    picked = picked.reshape(routes.shape[0], routes.shape[1], width).astype(jnp.float32)
    mixed = jnp.sum(route_weights[:, :, None] * picked, axis=1)
    moe_out = (residual.astype(jnp.float32) + mixed).astype(jnp.bfloat16)
    return (context, moe_out)


def solution(mesh):
    in_specs = (
        P("ctx", "exp"),
        P("ctx", "exp", None),
        P("ctx"),
        P("exp", None, "ctx"),
        P("exp", "ctx", None),
        P(("ctx", "exp"), None),
        P(("ctx", "exp"), None),
    )
    out_specs = (P("ctx", "exp"), P(("ctx", "exp"), None))
    return jax.shard_map(shards, mesh=mesh, in_specs=in_specs, out_specs=out_specs, check_vma=False)
```

profile of v0, /device:TPU:8, one launch (start us, length us, event | category | flops | bytes accessed | tf_op | source)
XLA Modules:
  0.0 310.8 jit_solution(5982555002560854336)
XLA Ops:
  7.2 0.7 all-gather.3.cloned.1.call-update
  8.0 0.5 copy-done
  8.5 14.4 %convolution_convert_fusion = bf16[1280,6144]{1,0:T(8,128)(2,1)} fusion(bf16[1,512,6144]{2,1,0:T(8,128)(2,1)} %param.11, bf16[1,1280,512]{2,1,0:T(8,128)(2,1)S(1)} %copy-done), kind=kOutput, calls=%fused_computation.1 | convolution fusion | flops 8060928000 | bytes 23330816 | tf_op jit(solution)/shard_map/dot_general | solution.py:59
  23.0 0.6 copy-done.4
  23.6 43.7 %all-gather = bf16[32,1,128]{2,1,0:T(2,128)(2,1)S(1)} all-gather(bf16[1,1,128]{2,1,0:T(2,128)(2,1)S(1)} %convert_bitcast_fusion.1), channel_id=1, replica_groups=mesh['ctx'=32,'exp'=8] {'ctx'}, dimensions={0}, use_global_device_ids=true | all-gather | bytes 8448 | tf_op jit(solution)/shard_map/all_gather | solution.py:19
  67.8 1.8 fusion.8
  69.7 23.1 %all-gather.3.cloned.1.call-done = bf16[4096,1,256]{2,0,1:T(8,128)(2,1)} async-done(((bf16[128,1,256]{2,0,1:T(8,128)(2,1)}), bf16[4096,1,256]{2,0,1:T(8,128)(2,1)}) %all-gather.3.cloned.1.call-update) | async-done | bytes 2097168 | tf_op jit(solution)/shard_map/all_gather | solution.py:18
  92.8 3.3 %fusion = (f32[6,128]{1,0:T(8,128)S(1)}, f32[4096,128,6]{1,0,2:T(8,128)S(1)}) fusion(pred[128,4096]{0,1:T(8,128)(4,1)S(1)} %fusion.8, bf16[128,6,128]{0,2,1:T(8,128)(2,1)S(1)} %bitcast.86, bf16[4096,1,256]{2,0,1:T(8,128)(2,1)} %all-gather.3.cloned.1.call-done), kind=kOutput, calls=%fused_computation.4 | convolution fusion | flops 814742784 | bytes 14355456 | tf_op jit(solution)/shard_map/qhgd,khd->hgqk/dot_general | solution.py:23
  96.1 3.1 fusion.1
  99.3 3.4 %fusion.17 = bf16[128,1,6,128]{0,3,2,1:T(8,128)(2,1)S(1)} fusion(bf16[4096,1,256]{2,0,1:T(8,128)(2,1)S(1)} %copy-done.5, f32[4096,128,6]{1,0,2:T(8,128)S(1)} %get-tuple-element.11, f32[6,128]{1,0:T(8,128)S(1)} %broadcast_maximum_fusion, pred[128,4096]{0,1:T(8,128)(4,1)S(1)} %fusion.8, f32[128,6]{0,1:T(8,128)S(1)} %bitcast.88), kind=kOutput, calls=%fused_computation.19 | convolution fusion | flops 821231616 | bytes 14360576 | tf_op jit(solution)/shard_map/hgqk,khd->qhgd/dot_general | solution.py:39
  102.6 0.2 copy.40
  102.8 0.9 convert_element_type.50
  103.8 5.7 %all-to-all-start = ((bf16[8,16,768]{2,1,0:T(8,128)(2,1)}), bf16[8,16,768]{2,1,0:T(8,128)(2,1)S(1)}, u32[]{:S(2)}, u32[]{:S(2)}) async-start(bf16[8,16,768]{2,1,0:T(8,128)(2,1)} %convert_element_type.50), calls=%async_computation | async-start | bytes 393216 | tf_op jit(solution)/shard_map/all_to_all | solution.py:50
  109.7 0.2 select_reduce_fusion
  109.9 173.7 %reduce-scatter.2.cloned.1.call-done = bf16[40,6144]{1,0:T(8,128)(2,1)} async-done(((bf16[1280,6144]{1,0:T(8,128)(2,1)}), bf16[40,6144]{1,0:T(8,128)(2,1)}) %reduce-scatter.2.cloned.1.call-update) | async-done | bytes 491536 | tf_op jit(solution)/shard_map/reduce_scatter | solution.py:58
  283.6 2.1 reshape.94
  285.7 5.8 %all-to-all-start.1 = ((bf16[8,5,6144]{2,1,0:T(8,128)(2,1)}), bf16[8,5,6144]{2,1,0:T(8,128)(2,1)S(1)}, u32[]{:S(2)}, u32[]{:S(2)}) async-start(bf16[8,5,6144]{2,1,0:T(8,128)(2,1)} %reshape.94), calls=%async_computation.2 | async-start | bytes 1572864 | tf_op jit(solution)/shard_map/all_to_all | solution.py:65
  291.7 0.8 copy.45
  292.6 8.0 %all-to-all-done.1 = bf16[8,5,6144]{2,1,0:T(8,128)(2,1)S(1)} async-done(((bf16[8,5,6144]{2,1,0:T(8,128)(2,1)}), bf16[8,5,6144]{2,1,0:T(8,128)(2,1)S(1)}, u32[]{:S(2)}, u32[]{:S(2)}) %all-to-all-start.1) | async-done | bytes 491552 | tf_op jit(solution)/shard_map/all_to_all | solution.py:65
  300.6 0.2 reshape.95
  300.8 0.8 gather_fusion
  301.6 0.5 reshape.97
  302.1 1.1 multiply_reduce_fusion
  303.2 0.7 add_convert_fusion
  (31 shorter events, 0.9 us)
Async XLA Ops:
  7.2 1.3 copy-start
  7.2 85.6 %all-gather.3.cloned.1.call-start = ((), (), s32[]{:S(2)}) async-start(), calls=%async_computation.3 | async-start | bytes 2162688 | tf_op jit(solution)/shard_map/all_gather | solution.py:18
  7.9 275.7 %reduce-scatter.2.cloned.1.call-start = ((), (), s32[]{:S(2)}) async-start(), calls=%async_computation.4 | async-start | bytes 16220160 | tf_op jit(solution)/shard_map/reduce_scatter | solution.py:58
  22.9 0.7 copy-start.4
  22.9 44.4 %copy-start.1 = (bf16[128,768]{1,0:T(8,128)(2,1)S(1)}, bf16[128,768]{1,0:T(8,128)(2,1)}, u32[]{:S(2)}) copy-start(bf16[128,768]{1,0:T(8,128)(2,1)} %param.7) | copy-start | bytes 589828
  22.9 44.6 %copy-start.2 = (s32[16,2]{0,1:T(2,128)S(1)}, s32[16,2]{0,1:T(2,128)}, u32[]{:S(2)}) copy-start(s32[16,2]{0,1:T(2,128)} %param.12) | copy-start | bytes 388
  92.8 6.5 %copy-start.5 = (bf16[4096,1,256]{2,0,1:T(8,128)(2,1)S(1)}, bf16[4096,1,256]{2,0,1:T(8,128)(2,1)}, u32[]{:S(2)}) copy-start(bf16[4096,1,256]{2,0,1:T(8,128)(2,1)} %all-gather.3.cloned.1.call-done) | copy-start | bytes 6291460
  99.2 192.3 %copy-start.3 = (f32[16,2]{0,1:T(2,128)S(1)}, f32[16,2]{0,1:T(2,128)}, u32[]{:S(2)}) copy-start(f32[16,2]{0,1:T(2,128)} %param.13) | copy-start | bytes 388
  103.8 182.0 %all-to-all-start = ((bf16[8,16,768]{2,1,0:T(8,128)(2,1)}), bf16[8,16,768]{2,1,0:T(8,128)(2,1)S(1)}, u32[]{:S(2)}, u32[]{:S(2)}) async-start(bf16[8,16,768]{2,1,0:T(8,128)(2,1)} %convert_element_type.50), calls=%async_computation | async-start | bytes 393216 | tf_op jit(solution)/shard_map/all_to_all | solution.py:50
  285.7 14.9 %all-to-all-start.1 = ((bf16[8,5,6144]{2,1,0:T(8,128)(2,1)}), bf16[8,5,6144]{2,1,0:T(8,128)(2,1)S(1)}, u32[]{:S(2)}, u32[]{:S(2)}) async-start(bf16[8,5,6144]{2,1,0:T(8,128)(2,1)} %reshape.94), calls=%async_computation.2 | async-start | bytes 1572864 | tf_op jit(solution)/shard_map/all_to_all | solution.py:65
Sparse Core Ops, SparseCore 0:
  10.8 81.9 all-gather.2
  97.4 186.1 reduce-scatter.1
where the time goes:
time: 311 us
  waiting for transfers between devices  206 us (66%)
  blocking collectives  43.7 us (14%)
  matrix products  21.2 us (7%)
  between operations  14.2 us (5%)
  starting transfers between devices  11.6 us (4%)
  local copies, waits for them, and re-layouts  7.36 us (2%)
  other arithmetic  7.13 us (2%)
    reduce_scatter x1, waiting for transfers between devices, shards(): lax.psum_scatter(jnp.dot(acts, weight, preferred_element_type=jnp.float32...  174 us
    all_gather x1, blocking collectives, shards(): doc_piece = lax.all_gather(doc_wire, 'ctx', axis=0, tiled=True)  43.7 us
    all_gather x1, waiting for transfers between devices, shards(): kv_piece = lax.all_gather(keys_values, 'ctx', axis=0, tiled=True)  23.1 us
    dot_general x1, matrix products, shards(): jnp.dot(acts, weight, preferred_element_type=jnp.float32)  14.4 us
    all_to_all x1, waiting for transfers between devices, shards(): lax.all_to_all(mine, 'exp', split_axis=0, concat_axis=0, tiled=True)  8.03 us
  transfers between devices with their start and end apart: 4, of which 3 were waited for; matrix products, arithmetic and copies ran while one was open for 10% of the time, Pallas kernels for 0%

commit v1 on v0

--- a/solution.py
+++ b/solution.py
@@ -15,7 +15,8 @@
     query_pos = first_pos + jnp.arange(tok_rows, dtype=jnp.int32)
     scale = 1.0 / math.sqrt(head_size)
     doc_wire = doc_ids.astype(jnp.bfloat16)
-    kv_piece = lax.all_gather(keys_values, "ctx", axis=0, tiled=True)
+    sent = jnp.stack([keys_values] * lax.axis_size("ctx"))
+    kv_piece = jnp.concatenate(lax.all_to_all(sent, "ctx", 0, 0), axis=0)
     doc_piece = lax.all_gather(doc_wire, "ctx", axis=0, tiled=True)
     count = kv_piece.shape[0]
     key_pos = jnp.arange(count, dtype=jnp.int32)

time: 311 us -> 242 us (0.78)
  waiting for transfers between devices: 206 us -> 84.7 us
  blocking collectives: 43.7 us -> 81.4 us
  starting transfers between devices: 11.6 us -> 22.2 us
    reduce_scatter x1, waiting for transfers between devices: 174 us -> 76.6 us  [shards(): lax.psum_scatter(jnp.dot(acts, weight, preferred_element_type=jnp.float32...]
    all_gather x1, blocking collectives: 43.7 us -> 81.4 us  [shards(): doc_piece = lax.all_gather(doc_wire, 'ctx', axis=0, tiled=True)]
    all_gather x1 -> x0, waiting for transfers between devices: 23.1 us -> none  [shards(): kv_piece = lax.all_gather(keys_values, 'ctx', axis=0, tiled=True)]
    all_to_all x0 -> x1, starting transfers between devices: none -> 10.7 us  [shards(): kv_piece = jnp.concatenate(lax.all_to_all(sent, 'ctx', 0, 0), axis=0)]
  transfers between devices with their start and end apart: 4 -> 4, of which waited for: 3 -> 2; matrix products, arithmetic and copies ran while one was open for 10% -> 8% of each run, Pallas kernels for 0% -> 0%
where the time goes in v1:
time: 242 us
  waiting for transfers between devices  84.7 us (35%)
  blocking collectives  81.4 us (34%)
  matrix products  22.3 us (9%)
  starting transfers between devices  22.2 us (9%)
  between operations  14.2 us (6%)
  local copies, waits for them, and re-layouts  9.86 us (4%)
  other arithmetic  7.12 us (3%)
    all_gather x1, blocking collectives, shards(): doc_piece = lax.all_gather(doc_wire, 'ctx', axis=0, tiled=True)  81.4 us
    reduce_scatter x1, waiting for transfers between devices, shards(): lax.psum_scatter(jnp.dot(acts, weight, preferred_element_type=jnp.float32...  76.6 us
    dot_general x1, matrix products, shards(): jnp.dot(acts, weight, preferred_element_type=jnp.float32)  14.4 us
    all_to_all x1, starting transfers between devices, shards(): kv_piece = jnp.concatenate(lax.all_to_all(sent, 'ctx', 0, 0), axis=0)  10.7 us
    all_to_all x1, waiting for transfers between devices, shards(): lax.all_to_all(mine, 'exp', split_axis=0, concat_axis=0, tiled=True)  8.03 us
    all_to_all x1, starting transfers between devices, shards(): lax.all_to_all(context, 'exp', split_axis=0, concat_axis=1, tiled=True)  5.75 us
    all_to_all x1, starting transfers between devices, shards(): lax.all_to_all(mine, 'exp', split_axis=0, concat_axis=0, tiled=True)  5.72 us
  transfers between devices with their start and end apart: 4, of which 2 were waited for; matrix products, arithmetic and copies ran while one was open for 8% of the time, Pallas kernels for 0%

profile of v1, /device:TPU:8, one launch (start us, length us, event | category | flops | bytes accessed | tf_op | source)
XLA Modules:
  0.0 241.8 jit_solution(10525211183050746185)
XLA Ops:
  7.2 1.3 copy-done
  8.5 14.4 %convolution_convert_fusion = bf16[1280,6144]{1,0:T(8,128)(2,1)} fusion(bf16[1,512,6144]{2,1,0:T(8,128)(2,1)} %param.11, bf16[1,1280,512]{2,1,0:T(8,128)(2,1)S(1)} %copy-done), kind=kOutput, calls=%fused_computation.1 | convolution fusion | flops 8060928000 | bytes 23330816 | tf_op jit(solution)/shard_map/dot_general | solution.py:60
  23.0 0.8 copy-done.2
  23.8 1.6 stack.2
  25.4 10.7 %all-to-all-start = ((bf16[32,128,1,256]{3,1,2,0:T(8,128)(2,1)}), bf16[32,128,1,256]{3,1,2,0:T(8,128)(2,1)}, u32[]{:S(2)}, u32[]{:S(2)}) async-start(bf16[32,128,1,256]{3,1,2,0:T(8,128)(2,1)} %stack.2), calls=%async_computation | async-start | bytes 4194304 | tf_op jit(solution)/shard_map/all_to_all | solution.py:19
  36.1 81.4 %all-gather = bf16[32,1,128]{2,1,0:T(2,128)(2,1)S(1)} all-gather(bf16[1,1,128]{2,1,0:T(2,128)(2,1)S(1)} %convert_bitcast_fusion.1), channel_id=1, replica_groups=mesh['ctx'=32,'exp'=8] {'ctx'}, dimensions={0}, use_global_device_ids=true | all-gather | bytes 8448 | tf_op jit(solution)/shard_map/all_gather | solution.py:20
  118.0 1.8 fusion.8
  119.9 3.2 %fusion = (f32[6,128]{1,0:T(8,128)S(1)}, f32[4096,128,6]{1,0,2:T(8,128)S(1)}) fusion(pred[128,4096]{0,1:T(8,128)(4,1)S(1)} %fusion.8, bf16[128,6,128]{0,2,1:T(8,128)(2,1)S(1)} %bitcast.88, bf16[4096,1,256]{2,0,1:T(8,128)(2,1)} %bitcast.3), kind=kOutput, calls=%fused_computation.4 | convolution fusion | flops 814742784 | bytes 14355456 | tf_op jit(solution)/shard_map/qhgd,khd->hgqk/dot_general | solution.py:24
  123.1 3.1 %fusion.1 = f32[6,128]{1,0:T(8,128)S(1)} fusion(f32[4096,128,6]{1,0,2:T(8,128)S(1)} %get-tuple-element.11, f32[6,128]{1,0:T(8,128)S(1)} %broadcast_maximum_fusion, pred[128,4096]{0,1:T(8,128)(4,1)S(1)} %fusion.8), kind=kLoop, calls=%fused_computation.5 | loop fusion | flops 15727872 | bytes 13113344 | tf_op jit(solution)/shard_map/reduce_sum | solution.py:39
  126.2 4.7 %fusion.17 = bf16[128,1,6,128]{0,3,2,1:T(8,128)(2,1)S(1)} fusion(bf16[4096,1,256]{2,0,1:T(8,128)(2,1)} %bitcast.3, f32[4096,128,6]{1,0,2:T(8,128)S(1)} %get-tuple-element.11, f32[6,128]{1,0:T(8,128)S(1)} %broadcast_maximum_fusion, pred[128,4096]{0,1:T(8,128)(4,1)S(1)} %fusion.8, f32[128,6]{0,1:T(8,128)S(1)} %bitcast.91), kind=kOutput, calls=%fused_computation.19 | convolution fusion | flops 821231616 | bytes 14358528 | tf_op jit(solution)/shard_map/hgqk,khd->qhgd/dot_general | solution.py:40
  130.9 0.2 copy.40
  131.1 0.9 convert_element_type.50
  132.0 5.7 %all-to-all-start.1 = ((bf16[8,16,768]{2,1,0:T(8,128)(2,1)}), bf16[8,16,768]{2,1,0:T(8,128)(2,1)S(1)}, u32[]{:S(2)}, u32[]{:S(2)}) async-start(bf16[8,16,768]{2,1,0:T(8,128)(2,1)} %convert_element_type.50), calls=%async_computation.1 | async-start | bytes 393216 | tf_op jit(solution)/shard_map/all_to_all | solution.py:51
  138.0 0.2 select_reduce_fusion
  138.2 76.6 %reduce-scatter.2.cloned.1.call-done = bf16[40,6144]{1,0:T(8,128)(2,1)} async-done(((bf16[1280,6144]{1,0:T(8,128)(2,1)}), bf16[40,6144]{1,0:T(8,128)(2,1)}) %reduce-scatter.2.cloned.1.call-update) | async-done | bytes 491536 | tf_op jit(solution)/shard_map/reduce_scatter | solution.py:59
  214.8 2.1 reshape.101
  216.9 5.7 %all-to-all-start.2 = ((bf16[8,5,6144]{2,1,0:T(8,128)(2,1)}), bf16[8,5,6144]{2,1,0:T(8,128)(2,1)S(1)}, u32[]{:S(2)}, u32[]{:S(2)}) async-start(bf16[8,5,6144]{2,1,0:T(8,128)(2,1)} %reshape.101), calls=%async_computation.3 | async-start | bytes 1572864 | tf_op jit(solution)/shard_map/all_to_all | solution.py:66
  222.8 0.8 copy.45
  223.7 8.0 %all-to-all-done.2 = bf16[8,5,6144]{2,1,0:T(8,128)(2,1)S(1)} async-done(((bf16[8,5,6144]{2,1,0:T(8,128)(2,1)}), bf16[8,5,6144]{2,1,0:T(8,128)(2,1)S(1)}, u32[]{:S(2)}, u32[]{:S(2)}) %all-to-all-start.2) | async-done | bytes 491552 | tf_op jit(solution)/shard_map/all_to_all | solution.py:66
  231.7 0.2 reshape.102
  231.9 0.8 gather_fusion
  232.7 0.5 reshape.104
  233.2 1.1 multiply_reduce_fusion
  234.3 0.7 add_convert_fusion
  (31 shorter events, 0.9 us)
Async XLA Ops:
  7.2 1.3 copy-start
  7.2 207.6 %reduce-scatter.2.cloned.1.call-start = ((), (), s32[]{:S(2)}) async-start(), calls=%async_computation.4 | async-start | bytes 16220160 | tf_op jit(solution)/shard_map/reduce_scatter | solution.py:59
  22.9 0.8 copy-start.2
  22.9 13.2 %copy-start.5 = (s32[128]{0:T(128)S(1)}, s32[128]{0:T(128)}, u32[]{:S(2)}) copy-start(s32[128]{0:T(128)} %param.9) | copy-start | bytes 1540
  22.9 94.6 %copy-start.1 = (bf16[128,768]{1,0:T(8,128)(2,1)S(1)}, bf16[128,768]{1,0:T(8,128)(2,1)}, u32[]{:S(2)}) copy-start(bf16[128,768]{1,0:T(8,128)(2,1)} %param.7) | copy-start | bytes 589828
  22.9 94.8 %copy-start.3 = (s32[16,2]{0,1:T(2,128)S(1)}, s32[16,2]{0,1:T(2,128)}, u32[]{:S(2)}) copy-start(s32[16,2]{0,1:T(2,128)} %param.12) | copy-start | bytes 388
  25.4 94.5 %all-to-all-start = ((bf16[32,128,1,256]{3,1,2,0:T(8,128)(2,1)}), bf16[32,128,1,256]{3,1,2,0:T(8,128)(2,1)}, u32[]{:S(2)}, u32[]{:S(2)}) async-start(bf16[32,128,1,256]{3,1,2,0:T(8,128)(2,1)} %stack.2), calls=%async_computation | async-start | bytes 4194304 | tf_op jit(solution)/shard_map/all_to_all | solution.py:19
  126.2 96.5 %copy-start.4 = (f32[16,2]{0,1:T(2,128)S(1)}, f32[16,2]{0,1:T(2,128)}, u32[]{:S(2)}) copy-start(f32[16,2]{0,1:T(2,128)} %param.13) | copy-start | bytes 388
  132.0 84.9 %all-to-all-start.1 = ((bf16[8,16,768]{2,1,0:T(8,128)(2,1)}), bf16[8,16,768]{2,1,0:T(8,128)(2,1)S(1)}, u32[]{:S(2)}, u32[]{:S(2)}) async-start(bf16[8,16,768]{2,1,0:T(8,128)(2,1)} %convert_element_type.50), calls=%async_computation.1 | async-start | bytes 393216 | tf_op jit(solution)/shard_map/all_to_all | solution.py:51
  216.9 14.7 %all-to-all-start.2 = ((bf16[8,5,6144]{2,1,0:T(8,128)(2,1)}), bf16[8,5,6144]{2,1,0:T(8,128)(2,1)S(1)}, u32[]{:S(2)}, u32[]{:S(2)}) async-start(bf16[8,5,6144]{2,1,0:T(8,128)(2,1)} %reshape.101), calls=%async_computation.3 | async-start | bytes 1572864 | tf_op jit(solution)/shard_map/all_to_all | solution.py:66
Sparse Core Ops, SparseCore 0:
  23.1 191.6 reduce-scatter.1
